TPU v7x, 32 devices: a whole 2x2x4 slice. The times are simulated.
32 devices in a mesh: member: 4 (over y, x), shard: 8 (over z, core).
Axes of the slice: x: 2, y: 2, z: 4, core: 2. Of those that a mesh axis runs over, the one named last changes fastest.
Arguments:
- trunk_out: bfloat16 [128, 8192], P('shard', 'member'), may hold values from -6 to 6
- segment_ids: int32 [128], replicated, may hold values from 0 to 7, never falling along the last dimension, each value on 1 to 32 neighbouring positions
- pair_order: int32 [8], replicated, may hold values from 0 to 7, each once
- w_query: bfloat16 [4, 8, 4096, 128], P('member', 'shard'), may hold values from -0.25 to 0.25
- w_key_value: bfloat16 [4, 8, 1024, 256], P('member', 'shard'), may hold values from -0.0625 to 0.0625
- w_out: bfloat16 [4, 512, 8192], P('member', 'shard'), may hold values from -0.25 to 0.25
- norm_gain: float32 [4, 8192], P('member'), may hold values from 0.1 to 1.9
- reward_weight: float32 [4, 8192], P('member'), may hold values from -0.0625 to 0.0625
Outputs:
- trunk_grad: float32 [128, 8192], P('member', 'shard')
- rewards: float32 [4, 8], P('member')
Inputs may be any that keep to these rules, and one draw needn't show every extreme that they name: `segment_ids`: segment numbers never fall along the tokens; every sequence 0 to 7 has 1 to 32 tokens, and one has exactly 32. Each sequence appears once; sequence pair_order[2 * i] is preferred to sequence pair_order[2 * i + 1].
All inputs are finite; a program needn't handle non-finite values.
Results may differ from a plain program's by a relative error of at most 0.011.
Values may be sent and summed in bfloat16 or wider, within the bound.
No kernel may reach another device: no remote copies, remote signals or barrier semaphores. Data moves between devices by JAX's collectives and lax.ppermute only.
A program may use at most 64 MiB of HBM per device.

v0:
```python
import math
import jax
import jax.numpy as jnp
from jax import lax
from jax.sharding import PartitionSpec as P

HD = 128
SEQS = 8
softcap_limit = 20.0
loss_scale = 256.0
norm_eps = 1e-05


def from_partner(block, axis, stride):
    count = lax.axis_size(axis)
    route = []
    for low in range(count):
        high = low | 1 << stride
        if high != low and high < count:
            route += [(low, high), (high, low)]
    return lax.ppermute(block, axis, route)


def partner_swap(values, bit_number):
    return from_partner(values, "shard", bit_number)


def group_total(values, bit_list):
    for bit_number in bit_list:
        values = values + partner_swap(values, bit_number)
    return values


def pair_join(own_part, other_part, pair_side, join_axis):
    first_part = jnp.where(pair_side == 0, own_part, other_part)
    second_part = jnp.where(pair_side == 0, other_part, own_part)
    return jnp.concatenate([first_part, second_part], axis=join_axis)


def on_device(
    trunk_out, segment_ids, pair_order, w_query, w_key_value, w_out, norm_gain, reward_weight
):
    n_shard = lax.axis_size("shard")
    query_heads = n_shard // 2
    kv_count = max(1, query_heads // 8)
    group_size = query_heads // kv_count
    shard_index = lax.axis_index("shard")
    pair_side = shard_index % 2
    head_index = shard_index // 2
    block_index = shard_index % (2 * group_size) // 2
    local_rows, local_width = trunk_out.shape
    features = lax.all_gather(trunk_out, "member", axis=1, tiled=True)
    gathered = lax.all_gather(features, "shard", axis=0, tiled=True)
    tok_count, model_width = gathered.shape
    half_width = model_width // 2
    half_rows = tok_count // 2
    half_head = HD // 2
    row_block = half_width // group_size
    scale_factor = 1.0 / math.sqrt(HD)
    group_bits = list(range((2 * group_size).bit_length() - 1))
    query_piece = w_query[0, 0]
    kv_piece = w_key_value[0, 0]
    out_rows = w_out[0]
    gain_vector = norm_gain[0]
    head_weight = reward_weight[0]
    positions = jnp.arange(tok_count)
    own_start = pair_side * half_rows
    own_positions = own_start + jnp.arange(half_rows)
    own_segments = lax.dynamic_slice_in_dim(segment_ids, own_start, half_rows, 0)
    allowed = (own_segments[:, None] == segment_ids[None, :]) & (
        positions[None, :] <= own_positions[:, None]
    )
    member_of = jnp.arange(SEQS)[:, None] == segment_ids[None, :]
    pooling = member_of.astype(jnp.bfloat16)
    lengths = jnp.sum(member_of.astype(jnp.float32), axis=1)
    own_pooling = lax.dynamic_slice_in_dim(pooling, own_start, half_rows, 1)
    half_features = lax.dynamic_slice_in_dim(gathered, pair_side * half_width, half_width, 1)
    query_partial = jnp.dot(half_features, query_piece, preferred_element_type=jnp.float32)
    kept_rows = lax.dynamic_slice_in_dim(query_partial, own_start, half_rows, 0)
    sent_rows = lax.dynamic_slice_in_dim(query_partial, half_rows - own_start, half_rows, 0)
    queries = (kept_rows + partner_swap(sent_rows, 0)).astype(jnp.bfloat16)
    kv_features = lax.dynamic_slice_in_dim(half_features, block_index * row_block, row_block, 1)
    kv_values = group_total(
        jnp.dot(kv_features, kv_piece, preferred_element_type=jnp.float32), group_bits
    ).astype(jnp.bfloat16)
    key_full = kv_values[:, :HD]
    value_full = kv_values[:, HD:]
    raw_scores = (
        jnp.einsum("td,sd->ts", queries, key_full, preferred_element_type=jnp.float32)
        * scale_factor
    )
    capped = softcap_limit * jnp.tanh(raw_scores / softcap_limit)
    weights_exp = jnp.where(allowed, jnp.exp(capped), 0.0)
    attention = weights_exp / jnp.sum(weights_exp, axis=1, keepdims=True)
    attention_low = attention.astype(jnp.bfloat16)
    attended = jnp.dot(attention_low, value_full, preferred_element_type=jnp.float32).astype(
        jnp.bfloat16
    )
    seq_part = jnp.dot(own_pooling, attended, preferred_element_type=jnp.float32)
    seq_total = seq_part + partner_swap(seq_part, 0)
    seq_mean = (seq_total / lengths[:, None]).astype(jnp.bfloat16)
    own_dims = lax.dynamic_slice_in_dim(seq_mean, pair_side * half_head, half_head, 1)
    head_part = jnp.dot(own_dims, out_rows, preferred_element_type=jnp.float32)
    pooled_attn = lax.psum(head_part, "shard")
    pooled_input = jnp.dot(pooling, gathered, preferred_element_type=jnp.float32) / lengths[:, None]
    hidden = pooled_input + pooled_attn
    inverse_rms = lax.rsqrt(jnp.mean(hidden * hidden, axis=1) + norm_eps)
    normed = hidden * inverse_rms[:, None] * gain_vector
    rewards = jnp.sum(normed * head_weight, axis=1)
    seq_ids = jnp.arange(SEQS)
    chosen = (pair_order[0::2][:, None] == seq_ids[None, :]).astype(jnp.float32)
    rejected = (pair_order[1::2][:, None] == seq_ids[None, :]).astype(jnp.float32)
    margin = jnp.sum(chosen * rewards, axis=1) - jnp.sum(rejected * rewards, axis=1)
    pair_slope = loss_scale * jax.nn.sigmoid(-margin)
    reward_grad = jnp.sum(rejected * pair_slope[:, None], axis=0) - jnp.sum(
        chosen * pair_slope[:, None], axis=0
    )
    scaled_grad = reward_grad[:, None] * head_weight * gain_vector
    hidden_grad = inverse_rms[:, None] * (
        scaled_grad
        - hidden * (inverse_rms**2)[:, None] * jnp.mean(hidden * scaled_grad, axis=1, keepdims=True)
    )
    per_token = hidden_grad / lengths[:, None]
    grad_low = hidden_grad.astype(jnp.bfloat16)
    grad_dims = (
        jnp.einsum("jd,ed->je", grad_low, out_rows, preferred_element_type=jnp.float32)
        / lengths[:, None]
    )
    mean_grad = pair_join(grad_dims, partner_swap(grad_dims, 0), pair_side, 1)
    out_grad = jnp.take(mean_grad, own_segments, axis=0).astype(jnp.bfloat16)
    prob_grad = jnp.einsum("td,sd->ts", out_grad, value_full, preferred_element_type=jnp.float32)
    score_grad = attention * (prob_grad - jnp.sum(attention * prob_grad, axis=1, keepdims=True))
    raw_grad = (score_grad * (1.0 - (capped / softcap_limit) ** 2) * scale_factor).astype(
        jnp.bfloat16
    )
    query_grad = jnp.dot(raw_grad, key_full, preferred_element_type=jnp.float32).astype(
        jnp.bfloat16
    )
    key_grad = jnp.einsum("ts,td->sd", raw_grad, queries, preferred_element_type=jnp.float32)
    value_grad = jnp.einsum(
        "ts,td->sd", attention_low, out_grad, preferred_element_type=jnp.float32
    )
    kv_grad = group_total(jnp.concatenate([key_grad, value_grad], axis=1), group_bits).astype(
        jnp.bfloat16
    )
    query_wire = lax.optimization_barrier(query_grad).astype(jnp.float32)
    query_all = pair_join(
        query_grad, partner_swap(query_wire, 0).astype(jnp.bfloat16), pair_side, 0
    )
    grad_half = jnp.einsum("td,rd->tr", query_all, query_piece, preferred_element_type=jnp.float32)
    kv_term = jnp.einsum("te,re->tr", kv_grad, kv_piece, preferred_element_type=jnp.float32)
    start_col = block_index * row_block
    grad_half = lax.dynamic_update_slice_in_dim(
        grad_half,
        lax.dynamic_slice_in_dim(grad_half, start_col, row_block, 1) + kv_term,
        start_col,
        1,
    )
    pair_rows = 2 * local_rows
    start_row = head_index * pair_rows
    pair_segments = lax.dynamic_slice_in_dim(segment_ids, start_row, pair_rows, 0)
    token_half = lax.dynamic_slice_in_dim(per_token, pair_side * half_width, half_width, 1)
    direct = jnp.take(token_half, pair_segments, axis=0)
    grad_half = lax.dynamic_update_slice_in_dim(
        grad_half,
        lax.dynamic_slice_in_dim(grad_half, start_row, pair_rows, 0) + direct,
        start_row,
        0,
    )
    by_member = lax.psum_scatter(grad_half, "member", scatter_dimension=0, tiled=True)
    member_rows = by_member.shape[0]
    placed = lax.dynamic_update_slice_in_dim(
        jnp.zeros((member_rows, model_width), jnp.float32), by_member, pair_side * half_width, 1
    )
    trunk_grad = lax.psum_scatter(placed, "shard", scatter_dimension=1, tiled=True)
    return (trunk_grad, rewards[None])


def solution(mesh):
    placed = (
        P("shard", "member"),
        P(),
        P(),
        P("member", "shard", None, None),
        P("member", "shard", None, None),
        P("member", "shard", None),
        P("member", None),
        P("member", None),
    )
    return jax.shard_map(
        on_device,
        mesh=mesh,
        in_specs=placed,
        out_specs=(P("member", "shard"), P("member", None)),
        check_vma=False,
    )
```

profile of v0, /device:TPU:0, one launch (start us, length us, event | category | flops | bytes accessed | tf_op | source)
XLA Modules:
  0.0 226.3 jit_solution(8891735521188320311)
XLA Ops:
  7.2 12.1 %all_gather.6 = bf16[16,8192]{1,0:T(8,128)(2,1)} all-gather(bf16[16,2048]{1,0:T(8,128)(2,1)} %param.8), channel_id=1, replica_groups=mesh['member'=4,'shard'=8] {'member'}, dimensions={1}, use_global_device_ids=true | all-gather | bytes 327680 | tf_op jit(solution)/shard_map/all_gather | solution.py:52
  19.5 0.7 compare_and_fusion.1
  20.3 0.7 iota_compare_fusion.1
  20.9 28.0 %all-gather.2.cloned.1.call-done = bf16[128,8192]{1,0:T(8,128)(2,1)} async-done(((bf16[16,8192]{1,0:T(8,128)(2,1)}), bf16[128,8192]{1,0:T(8,128)(2,1)}) %all-gather.2.cloned.1.call-update) | async-done | bytes 2097168 | tf_op jit(solution)/shard_map/all_gather | solution.py:53
  49.0 1.4 fusion.13
  50.7 1.6 fusion.9
  52.4 1.5 collective-permute-start.2
  53.9 4.2 %collective-permute-done.2 = f32[128,256]{1,0:T(8,128)S(1)} collective-permute-done((f32[128,256]{1,0:T(8,128)S(1)}, f32[128,256]{1,0:T(8,128)S(1)}, u32[]{:S(2)}, u32[]{:S(2)}) %collective-permute-start.2) | collective-permute-done | bytes 131104 | tf_op jit(solution)/shard_map/ppermute | solution.py:21
  58.2 1.9 collective-permute-start.3
  60.0 6.7 %collective-permute-done.3 = f32[128,256]{1,0:T(8,128)S(1)} collective-permute-done((f32[128,256]{1,0:T(8,128)S(1)}, f32[128,256]{1,0:T(8,128)S(1)}, u32[]{:S(2)}, u32[]{:S(2)}) %collective-permute-start.3) | collective-permute-done | bytes 131104 | tf_op jit(solution)/shard_map/ppermute | solution.py:21
  67.5 1.0 collective-permute-done.4
  68.7 2.2 fusion.5
  71.3 54.7 %all-reduce.2.cloned.1.call-done = f32[8,8192]{1,0:T(8,128)} async-done(((f32[8,8192]{1,0:T(8,128)}), f32[8,8192]{1,0:T(8,128)}) %all-reduce.2.cloned.1.call-update) | async-done | bytes 262160 | tf_op jit(solution)/shard_map/psum | solution.py:104
  126.0 1.5 multiply_reduce_fusion.2
  129.0 1.5 gather_fusion.1
  132.9 0.8 collective-permute-done.7
  134.4 5.2 %collective-permute-done.8 = f32[128,256]{0,1:T(8,128)S(1)} collective-permute-done((f32[128,256]{0,1:T(8,128)S(1)}, f32[128,256]{0,1:T(8,128)S(1)}, u32[]{:S(2)}, u32[]{:S(2)}) %collective-permute-start.8) | collective-permute-done | bytes 131104 | tf_op jit(solution)/shard_map/ppermute | solution.py:21
  139.6 1.5 collective-permute-start.9
  141.6 6.7 %collective-permute-done.9 = f32[128,256]{0,1:T(8,128)S(1)} collective-permute-done((f32[128,256]{0,1:T(8,128)S(1)}, f32[128,256]{0,1:T(8,128)S(1)}, u32[]{:S(2)}, u32[]{:S(2)}) %collective-permute-start.9) | collective-permute-done | bytes 131104 | tf_op jit(solution)/shard_map/ppermute | solution.py:21
  148.7 1.3 copy-done.1
  150.1 34.3 %reduce-scatter.3.cloned.1.call-done = f32[32,4096]{1,0:T(8,128)} async-done(((f32[128,4096]{1,0:T(8,128)}), f32[32,4096]{1,0:T(8,128)}) %reduce-scatter.3.cloned.1.call-update) | async-done | bytes 524304 | tf_op jit(solution)/shard_map/reduce_scatter | solution.py:170
  184.5 1.1 constant_dynamic-update-slice_fusion
  185.6 1.0 copy-done.4
  186.6 33.2 %reduce-scatter.5.cloned.1.call-done = f32[32,1024]{1,0:T(8,128)} async-done(((f32[32,8192]{1,0:T(8,128)}), f32[32,1024]{1,0:T(8,128)}) %reduce-scatter.5.cloned.1.call-update) | async-done | bytes 131088 | tf_op jit(solution)/shard_map/reduce_scatter | solution.py:175
  (84 shorter events, 7.1 us)
Async XLA Ops:
  7.2 43.5 %copy-start = (bf16[1,1,4096,128]{3,2,1,0:T(8,128)(2,1)S(1)}, bf16[1,1,4096,128]{3,2,1,0:T(8,128)(2,1)}, u32[]{:S(2)}) copy-start(bf16[1,1,4096,128]{3,2,1,0:T(8,128)(2,1)} %param.11) | copy-start | bytes 3145732
  7.2 41.8 %all-gather.2.cloned.1.call-start = ((), (), s32[]{:S(2)}) async-start(), calls=%async_computation.2 | async-start | bytes 2359296 | tf_op jit(solution)/shard_map/all_gather | solution.py:53
  19.4 106.6 %all-reduce.2.cloned.1.call-start = ((), (), s32[]{:S(2)}) async-start(), calls=%async_computation.3 | async-start | bytes 524288 | tf_op jit(solution)/shard_map/psum | solution.py:104
  20.9 45.9 %copy-start.9 = (s32[128]{0:T(128)S(1)}, s32[128]{0:T(128)}, u32[]{:S(2)}) copy-start(s32[128]{0:T(128)} %param.9) | copy-start | bytes 1540
  50.4 2.0 collective-permute-start.1
  52.3 18.7 %copy-start.11 = (s32[8]{0:T(128)S(1)}, s32[8]{0:T(128)}, u32[]{:S(2)}) copy-start(s32[8]{0:T(128)} %param.10) | copy-start | bytes 100
  52.3 73.6 %copy-start.2 = (bf16[128,8192]{1,0:T(8,128)(2,1)S(1)}, bf16[128,8192]{1,0:T(8,128)(2,1)}, u32[]{:S(2)}) copy-start(bf16[128,8192]{1,0:T(8,128)(2,1)} %all-gather.2.cloned.1.call-done) | copy-start | bytes 6291460
  52.4 5.8 %collective-permute-start.2 = (f32[128,256]{1,0:T(8,128)S(1)}, f32[128,256]{1,0:T(8,128)S(1)}, u32[]{:S(2)}, u32[]{:S(2)}) collective-permute-start(f32[128,256]{1,0:T(8,128)S(1)} %add.127), channel_id=1, source_target_pairs={{0,2},{2,0},{1,3},{3,1},{4,6},{6,4},{5,7},{7,5},{8,10},{10,8},{9,1... | collective-permute-start | bytes 393224 | tf_op jit(solution)/shard_map/ppermute | solution.py:21
  53.9 6.1 %collective-permute-start = (f32[64,128]{1,0:T(8,128)S(1)}, f32[64,128]{1,0:T(8,128)S(1)}, u32[]{:S(2)}, u32[]{:S(2)}) collective-permute-start(f32[64,128]{1,0:T(8,128)S(1)} %constant_dynamic-slice_fusion.1), channel_id=1, source_target_pairs={{0,1},{1,0},{2,3},{3,2},{4,5},{5,4},{6,7},{7,6},{8,9},{9,8},{10,11... | collective-permute-start | bytes 98312 | tf_op jit(solution)/shard_map/ppermute | solution.py:21
  58.2 8.6 %collective-permute-start.3 = (f32[128,256]{1,0:T(8,128)S(1)}, f32[128,256]{1,0:T(8,128)S(1)}, u32[]{:S(2)}, u32[]{:S(2)}) collective-permute-start(f32[128,256]{1,0:T(8,128)S(1)} %add.128), channel_id=1, source_target_pairs={{0,4},{4,0},{1,5},{5,1},{2,6},{6,2},{3,7},{7,3},{8,12},{12,8},{9,1... | collective-permute-start | bytes 393224 | tf_op jit(solution)/shard_map/ppermute | solution.py:21
  67.4 1.2 collective-permute-start.4
  68.7 58.9 %copy-start.7 = (f32[1,8192]{1,0:T(1,128)S(1)}, f32[1,8192]{1,0:T(1,128)}, u32[]{:S(2)}) copy-start(f32[1,8192]{1,0:T(1,128)} %param.15) | copy-start | bytes 98308
  68.7 58.9 %copy-start.8 = (f32[1,8192]{1,0:T(1,128)S(1)}, f32[1,8192]{1,0:T(1,128)}, u32[]{:S(2)}) copy-start(f32[1,8192]{1,0:T(1,128)} %param.14) | copy-start | bytes 98308
  70.9 113.5 %reduce-scatter.3.cloned.1.call-start = ((), (), s32[]{:S(2)}) async-start(), calls=%async_computation.4 | async-start | bytes 2621440 | tf_op jit(solution)/shard_map/reduce_scatter | solution.py:170
  126.0 2.6 %copy-start.3 = (bf16[1,64,8192]{2,1,0:T(8,128)(2,1)S(1)}, bf16[1,64,8192]{2,1,0:T(8,128)(2,1)}, u32[]{:S(2)}) copy-start(bf16[1,64,8192]{2,1,0:T(8,128)(2,1)} %param.13) | copy-start | bytes 3145732
  127.8 2.7 %copy-start.10 = (f32[8]{0:T(128)}, f32[8]{0:T(128)S(1)}, u32[]{:S(2)}) copy-start(f32[8]{0:T(128)S(1)} %multiply_reduce_fusion.1) | copy-start | bytes 100
  128.9 1.6 collective-permute-start.5
  132.2 16.1 %copy-start.6 = (bf16[1,1,1024,256]{3,2,1,0:T(8,128)(2,1)S(1)}, bf16[1,1,1024,256]{3,2,1,0:T(8,128)(2,1)}, u32[]{:S(2)}) copy-start(bf16[1,1,1024,256]{3,2,1,0:T(8,128)(2,1)} %param.12) | copy-start | bytes 1572868
  132.2 1.5 collective-permute-start.7
  132.9 1.5 collective-permute-start.6
  133.7 5.8 %collective-permute-start.8 = (f32[128,256]{0,1:T(8,128)S(1)}, f32[128,256]{0,1:T(8,128)S(1)}, u32[]{:S(2)}, u32[]{:S(2)}) collective-permute-start(f32[128,256]{0,1:T(8,128)S(1)} %fusion.40), channel_id=1, source_target_pairs={{0,2},{2,0},{1,3},{3,1},{4,6},{6,4},{5,7},{7,5},{8,10},{10,8},{9,1... | collective-permute-start | bytes 393224 | tf_op jit(solution)/shard_map/ppermute | solution.py:21
  139.6 8.7 %collective-permute-start.9 = (f32[128,256]{0,1:T(8,128)S(1)}, f32[128,256]{0,1:T(8,128)S(1)}, u32[]{:S(2)}, u32[]{:S(2)}) collective-permute-start(f32[128,256]{0,1:T(8,128)S(1)} %add.137), channel_id=1, source_target_pairs={{0,4},{4,0},{1,5},{5,1},{2,6},{6,2},{3,7},{7,3},{8,12},{12,8},{9,1... | collective-permute-start | bytes 393224 | tf_op jit(solution)/shard_map/ppermute | solution.py:21
  141.1 7.5 %copy-start.5 = (f32[32,4096]{1,0:T(8,128)S(1)}, f32[32,4096]{1,0:T(8,128)}, u32[]{:S(2)}) copy-start(f32[32,4096]{1,0:T(8,128)} %gather_fusion.1) | copy-start | bytes 1572868
  150.1 69.7 %reduce-scatter.5.cloned.1.call-start = ((), (), s32[]{:S(2)}) async-start(), calls=%async_computation.5 | async-start | bytes 1179648 | tf_op jit(solution)/shard_map/reduce_scatter | solution.py:175
  (2 other events, 2.3 us)
Sparse Core Ops, SparseCore 0:
  19.5 29.4 all-gather.1
  71.0 54.8 all-reduce.1
  150.2 34.1 reduce-scatter.2
  187.1 32.6 reduce-scatter.4
where the time goes:
time: 227 us; the launch traced here: 226 us
  waiting for transfers between devices  175 us (77%)
  between operations  14.1 us (6%)
  blocking collectives  12.1 us (5%)
  matrix products  9.47 us (4%)
  starting transfers between devices  6.59 us (3%)
  local copies, waits for them, and re-layouts  5.82 us (3%)
  other arithmetic  3.18 us (1%)
    psum x1, waiting for transfers between devices, on_device(): pooled_attn = lax.psum(head_part, 'shard')  54.7 us
    reduce_scatter x1, waiting for transfers between devices, on_device(): lax.psum_scatter(grad_half, 'member', scatter_dimension=0, tiled=True)  34.3 us
    reduce_scatter x1, waiting for transfers between devices, on_device(): lax.psum_scatter(placed, 'shard', scatter_dimension=1, tiled=True)  33.2 us
    all_gather x1, waiting for transfers between devices, on_device(): gathered = lax.all_gather(features, 'shard', axis=0, tiled=True)  28 us
    ppermute x10, waiting for transfers between devices, from_partner(): return lax.ppermute(block, axis, route)  24.7 us
    all_gather x1, blocking collectives, on_device(): features = lax.all_gather(trunk_out, 'member', axis=1, tiled=True)  12.1 us
    ppermute x10, starting transfers between devices, from_partner(): return lax.ppermute(block, axis, route)  6.43 us
  transfers between devices with their start and end apart: 14, of which 10 were waited for; matrix products, arithmetic and copies ran while one was open for 2% of the time, Pallas kernels for 0%

commit v1 on v0

--- a/solution.py
+++ b/solution.py
@@ -9,6 +9,18 @@
 softcap_limit = 20.0
 loss_scale = 256.0
 norm_eps = 1e-05
+
+
+def collect(x, axis, dim):
+    ways, here, turn = (lax.axis_size(axis), lax.axis_index(axis), x.shape[dim])
+    line, have = (x, 1)
+    while have < ways:
+        line = jnp.concatenate(
+            [line, lax.ppermute(line, axis, [(d, (d - have) % ways) for d in range(ways)])],
+            axis=dim,
+        )
+        have = 2 * have
+    return jnp.roll(line, here * turn, axis=dim)
 
 
 def from_partner(block, axis, stride):
@@ -50,7 +62,7 @@
     block_index = shard_index % (2 * group_size) // 2
     local_rows, local_width = trunk_out.shape
     features = lax.all_gather(trunk_out, "member", axis=1, tiled=True)
-    gathered = lax.all_gather(features, "shard", axis=0, tiled=True)
+    gathered = collect(features, "shard", 0)
     tok_count, model_width = gathered.shape
     half_width = model_width // 2
     half_rows = tok_count // 2

time: 227 us -> 269 us (1.19)
  waiting for transfers between devices: 175 us -> 209 us
  local copies, waits for them, and re-layouts: 5.82 us -> 12.5 us
    ppermute x0 -> x3, waiting for transfers between devices: none -> 60.3 us  [collect(): lax.ppermute(line, axis, [(d, (d - have) % ways) for d in range(ways)])]
    all_gather x1 -> x0, waiting for transfers between devices: 28 us -> none  [on_device(): gathered = lax.all_gather(features, 'shard', axis=0, tiled=True)]
    unnamed x24 -> x29, local copies, waits for them, and re-layouts: 2.35 us -> 7.94 us
    ppermute x0 -> x3, starting transfers between devices: none -> 4.55 us  [collect(): lax.ppermute(line, axis, [(d, (d - have) % ways) for d in range(ways)])]
  transfers between devices with their start and end apart: 14 -> 16, of which waited for: 10 -> 12; matrix products, arithmetic and copies ran while one was open for 2% -> 3% of each run, Pallas kernels for 0% -> 0%
where the time goes in v1:
time: 269 us
  waiting for transfers between devices  209 us (78%)
  between operations  14 us (5%)
  local copies, waits for them, and re-layouts  12.5 us (5%)
  blocking collectives  10.9 us (4%)
  matrix products  9.97 us (4%)
  starting transfers between devices  9.1 us (3%)
  other arithmetic  3.27 us (1%)
    ppermute x3, waiting for transfers between devices, collect(): lax.ppermute(line, axis, [(d, (d - have) % ways) for d in range(ways)])  60.3 us
    psum x1, waiting for transfers between devices, on_device(): pooled_attn = lax.psum(head_part, 'shard')  54 us
    reduce_scatter x1, waiting for transfers between devices, on_device(): lax.psum_scatter(grad_half, 'member', scatter_dimension=0, tiled=True)  34.3 us
    reduce_scatter x1, waiting for transfers between devices, on_device(): lax.psum_scatter(placed, 'shard', scatter_dimension=1, tiled=True)  33.4 us
    ppermute x10, waiting for transfers between devices, from_partner(): return lax.ppermute(block, axis, route)  26.9 us
    all_gather x1, blocking collectives, on_device(): features = lax.all_gather(trunk_out, 'member', axis=1, tiled=True)  10.9 us
    unnamed x29, local copies, waits for them, and re-layouts  7.94 us
  transfers between devices with their start and end apart: 16, of which 12 were waited for; matrix products, arithmetic and copies ran while one was open for 3% of the time, Pallas kernels for 0%

profile of v1, /device:TPU:0, one launch (start us, length us, event | category | flops | bytes accessed | tf_op | source)
XLA Modules:
  0.0 268.6 jit_solution(5610089000873011667)
XLA Ops:
  7.2 10.9 %all_gather.3 = bf16[16,8192]{1,0:T(8,128)(2,1)S(1)} all-gather(bf16[16,2048]{1,0:T(8,128)(2,1)} %param.8), channel_id=1, replica_groups=mesh['member'=4,'shard'=8] {'member'}, dimensions={1}, use_global_device_ids=true | all-gather | bytes 327680 | tf_op jit(solution)/shard_map/all_gather | solution.py:64
  18.1 1.3 collective-permute-start
  20.9 2.4 collective-permute-done
  23.3 2.4 collective-permute-start.1
  26.4 11.4 %collective-permute-done.1 = bf16[32,8192]{1,0:T(8,128)(2,1)S(1)} collective-permute-done((bf16[32,8192]{1,0:T(8,128)(2,1)S(1)}, bf16[32,8192]{1,0:T(8,128)(2,1)S(1)}, u32[]{:S(2)}, u32[]{:S(2)}) %collective-permute-start.1) | collective-permute-done | bytes 524320 | tf_op jit(solution)/shard_map/ppermute | solution.py:19
  40.3 46.4 %collective-permute-done.2 = bf16[64,8192]{1,0:T(8,128)(2,1)S(1)} collective-permute-done((bf16[64,8192]{1,0:T(8,128)(2,1)S(1)}, bf16[64,8192]{1,0:T(8,128)(2,1)S(1)}, u32[]{:S(2)}, u32[]{:S(2)}) %collective-permute-start.2) | collective-permute-done | bytes 1048608 | tf_op jit(solution)/shard_map/ppermute | solution.py:19
  86.7 1.1 constant_dynamic-update-slice_fusion.4
  90.1 1.1 constant_dynamic-update-slice_fusion
  91.1 1.3 fusion.14
  92.5 1.9 fusion.10
  95.1 5.3 %collective-permute-done.5 = f32[128,256]{1,0:T(8,128)S(1)} collective-permute-done((f32[128,256]{1,0:T(8,128)S(1)}, f32[128,256]{1,0:T(8,128)S(1)}, u32[]{:S(2)}, u32[]{:S(2)}) %collective-permute-start.5) | collective-permute-done | bytes 131104 | tf_op jit(solution)/shard_map/ppermute | solution.py:33
  101.4 7.8 %collective-permute-done.6 = f32[128,256]{1,0:T(8,128)S(1)} collective-permute-done((f32[128,256]{1,0:T(8,128)S(1)}, f32[128,256]{1,0:T(8,128)S(1)}, u32[]{:S(2)}, u32[]{:S(2)}) %collective-permute-start.6) | collective-permute-done | bytes 131104 | tf_op jit(solution)/shard_map/ppermute | solution.py:33
  111.1 1.0 fusion.6
  112.5 54.0 %all-reduce.2.cloned.1.call-done = f32[8,8192]{1,0:T(8,128)} async-done(((f32[8,8192]{1,0:T(8,128)}), f32[8,8192]{1,0:T(8,128)}) %all-reduce.2.cloned.1.call-update) | async-done | bytes 262160 | tf_op jit(solution)/shard_map/psum | solution.py:116
  166.5 2.1 multiply_reduce_fusion.2
  170.1 1.5 gather_fusion.1
  175.5 5.2 %collective-permute-done.11 = f32[128,256]{0,1:T(8,128)S(1)} collective-permute-done((f32[128,256]{0,1:T(8,128)S(1)}, f32[128,256]{0,1:T(8,128)S(1)}, u32[]{:S(2)}, u32[]{:S(2)}) %collective-permute-start.11) | collective-permute-done | bytes 131104 | tf_op jit(solution)/shard_map/ppermute | solution.py:33
  180.7 1.5 collective-permute-start.12
  182.6 6.7 %collective-permute-done.12 = f32[128,256]{0,1:T(8,128)S(1)} collective-permute-done((f32[128,256]{0,1:T(8,128)S(1)}, f32[128,256]{0,1:T(8,128)S(1)}, u32[]{:S(2)}, u32[]{:S(2)}) %collective-permute-start.12) | collective-permute-done | bytes 131104 | tf_op jit(solution)/shard_map/ppermute | solution.py:33
  189.3 1.4 fusion.2
  190.8 1.3 copy-done.1
  192.2 34.3 %reduce-scatter.3.cloned.1.call-done = f32[32,4096]{1,0:T(8,128)} async-done(((f32[128,4096]{1,0:T(8,128)}), f32[32,4096]{1,0:T(8,128)}) %reduce-scatter.3.cloned.1.call-update) | async-done | bytes 524304 | tf_op jit(solution)/shard_map/reduce_scatter | solution.py:182
  226.6 1.1 constant_dynamic-update-slice_fusion.8
  228.7 33.4 %reduce-scatter.5.cloned.1.call-done = f32[32,1024]{1,0:T(8,128)} async-done(((f32[32,8192]{1,0:T(8,128)}), f32[32,1024]{1,0:T(8,128)}) %reduce-scatter.5.cloned.1.call-update) | async-done | bytes 131088 | tf_op jit(solution)/shard_map/reduce_scatter | solution.py:187
  (95 shorter events, 17.9 us)
Async XLA Ops:
  7.2 85.3 %copy-start = (bf16[1,1,4096,128]{3,2,1,0:T(8,128)(2,1)S(1)}, bf16[1,1,4096,128]{3,2,1,0:T(8,128)(2,1)}, u32[]{:S(2)}) copy-start(bf16[1,1,4096,128]{3,2,1,0:T(8,128)(2,1)} %param.11) | copy-start | bytes 3145732
  7.2 159.3 %all-reduce.2.cloned.1.call-start = ((), (), s32[]{:S(2)}) async-start(), calls=%async_computation.2 | async-start | bytes 524288 | tf_op jit(solution)/shard_map/psum | solution.py:116
  18.1 5.2 %collective-permute-start = (bf16[16,8192]{1,0:T(8,128)(2,1)S(1)}, bf16[16,8192]{1,0:T(8,128)(2,1)S(1)}, u32[]{:S(2)}, u32[]{:S(2)}) collective-permute-start(bf16[16,8192]{1,0:T(8,128)(2,1)S(1)} %all_gather.3), channel_id=1, source_target_pairs={{0,7},{1,0},{2,1},{3,2},{4,3},{5,4},{6,5},{7,6},{8,15},{9,8},{10,9... | collective-permute-start | bytes 786440 | tf_op jit(solution)/shard_map/ppermute | solution.py:19
  23.3 14.4 %collective-permute-start.1 = (bf16[32,8192]{1,0:T(8,128)(2,1)S(1)}, bf16[32,8192]{1,0:T(8,128)(2,1)S(1)}, u32[]{:S(2)}, u32[]{:S(2)}) collective-permute-start(bf16[32,8192]{1,0:T(8,128)(2,1)S(1)} %pad_maximum_fusion.1), channel_id=1, source_target_pairs={{0,6},{1,7},{2,0},{3,1},{4,2},{5,3},{6,4},{7,5},{8,14},{9,15},{10,... | collective-permute-start | bytes 1572872 | tf_op jit(solution)/shard_map/ppermute | solution.py:19
  37.9 53.3 %copy-start.5 = (bf16[1,1,1024,256]{3,2,1,0:T(8,128)(2,1)S(1)}, bf16[1,1,1024,256]{3,2,1,0:T(8,128)(2,1)}, u32[]{:S(2)}) copy-start(bf16[1,1,1024,256]{3,2,1,0:T(8,128)(2,1)} %param.12) | copy-start | bytes 1572868
  37.9 48.9 %collective-permute-start.2 = (bf16[64,8192]{1,0:T(8,128)(2,1)S(1)}, bf16[64,8192]{1,0:T(8,128)(2,1)S(1)}, u32[]{:S(2)}, u32[]{:S(2)}) collective-permute-start(bf16[64,8192]{1,0:T(8,128)(2,1)S(1)} %pad_maximum_fusion), channel_id=1, source_target_pairs={{0,4},{1,5},{2,6},{3,7},{4,0},{5,1},{6,2},{7,3},{8,12},{9,13},{10,... | collective-permute-start | bytes 3145736 | tf_op jit(solution)/shard_map/ppermute | solution.py:19
  87.8 21.5 %copy-start.8 = (s32[128]{0:T(128)S(1)}, s32[128]{0:T(128)}, u32[]{:S(2)}) copy-start(s32[128]{0:T(128)} %param.9) | copy-start | bytes 1540
  88.5 22.6 %copy-start.2 = (bf16[1,64,8192]{2,1,0:T(8,128)(2,1)S(1)}, bf16[1,64,8192]{2,1,0:T(8,128)(2,1)}, u32[]{:S(2)}) copy-start(bf16[1,64,8192]{2,1,0:T(8,128)(2,1)} %param.13) | copy-start | bytes 3145732
  90.1 22.2 %copy-start.10 = (s32[8]{0:T(128)S(1)}, s32[8]{0:T(128)}, u32[]{:S(2)}) copy-start(s32[8]{0:T(128)} %param.10) | copy-start | bytes 100
  92.4 76.2 %copy-start.6 = (f32[1,8192]{1,0:T(1,128)S(1)}, f32[1,8192]{1,0:T(1,128)}, u32[]{:S(2)}) copy-start(f32[1,8192]{1,0:T(1,128)} %param.15) | copy-start | bytes 98308
  92.4 76.2 %copy-start.7 = (f32[1,8192]{1,0:T(1,128)S(1)}, f32[1,8192]{1,0:T(1,128)}, u32[]{:S(2)}) copy-start(f32[1,8192]{1,0:T(1,128)} %param.14) | copy-start | bytes 98308
  92.4 2.0 collective-permute-start.4
  94.5 6.0 %collective-permute-start.5 = (f32[128,256]{1,0:T(8,128)S(1)}, f32[128,256]{1,0:T(8,128)S(1)}, u32[]{:S(2)}, u32[]{:S(2)}) collective-permute-start(f32[128,256]{1,0:T(8,128)S(1)} %add.141), channel_id=1, source_target_pairs={{0,2},{2,0},{1,3},{3,1},{4,6},{6,4},{5,7},{7,5},{8,10},{10,8},{9,1... | collective-permute-start | bytes 393224 | tf_op jit(solution)/shard_map/ppermute | solution.py:33
  94.6 6.8 %collective-permute-start.3 = (f32[64,128]{1,0:T(8,128)S(1)}, f32[64,128]{1,0:T(8,128)S(1)}, u32[]{:S(2)}, u32[]{:S(2)}) collective-permute-start(f32[64,128]{1,0:T(8,128)S(1)} %constant_dynamic-slice_fusion.1), channel_id=1, source_target_pairs={{0,1},{1,0},{2,3},{3,2},{4,5},{5,4},{6,7},{7,6},{8,9},{9,8},{10,11... | collective-permute-start | bytes 98312 | tf_op jit(solution)/shard_map/ppermute | solution.py:33
  100.4 8.8 %collective-permute-start.6 = (f32[128,256]{1,0:T(8,128)S(1)}, f32[128,256]{1,0:T(8,128)S(1)}, u32[]{:S(2)}, u32[]{:S(2)}) collective-permute-start(f32[128,256]{1,0:T(8,128)S(1)} %add.142), channel_id=1, source_target_pairs={{0,4},{4,0},{1,5},{5,1},{2,6},{6,2},{3,7},{7,3},{8,12},{12,8},{9,1... | collective-permute-start | bytes 393224 | tf_op jit(solution)/shard_map/ppermute | solution.py:33
  109.9 1.2 collective-permute-start.7
  112.2 114.3 %reduce-scatter.3.cloned.1.call-start = ((), (), s32[]{:S(2)}) async-start(), calls=%async_computation.3 | async-start | bytes 2621440 | tf_op jit(solution)/shard_map/reduce_scatter | solution.py:182
  170.0 1.6 collective-permute-start.8
  172.3 18.4 %copy-start.4 = (f32[32,4096]{1,0:T(8,128)S(1)}, f32[32,4096]{1,0:T(8,128)}, u32[]{:S(2)}) copy-start(f32[32,4096]{1,0:T(8,128)} %gather_fusion.1) | copy-start | bytes 1572868
  173.3 1.6 collective-permute-start.10
  173.9 1.5 collective-permute-start.9
  174.8 5.8 %collective-permute-start.11 = (f32[128,256]{0,1:T(8,128)S(1)}, f32[128,256]{0,1:T(8,128)S(1)}, u32[]{:S(2)}, u32[]{:S(2)}) collective-permute-start(f32[128,256]{0,1:T(8,128)S(1)} %fusion.40), channel_id=1, source_target_pairs={{0,2},{2,0},{1,3},{3,1},{4,6},{6,4},{5,7},{7,5},{8,10},{10,8},{9,1... | collective-permute-start | bytes 393224 | tf_op jit(solution)/shard_map/ppermute | solution.py:33
  180.7 8.7 %collective-permute-start.12 = (f32[128,256]{0,1:T(8,128)S(1)}, f32[128,256]{0,1:T(8,128)S(1)}, u32[]{:S(2)}, u32[]{:S(2)}) collective-permute-start(f32[128,256]{0,1:T(8,128)S(1)} %add.151), channel_id=1, source_target_pairs={{0,4},{4,0},{1,5},{5,1},{2,6},{6,2},{3,7},{7,3},{8,12},{12,8},{9,1... | collective-permute-start | bytes 393224 | tf_op jit(solution)/shard_map/ppermute | solution.py:33
  192.2 69.8 %reduce-scatter.5.cloned.1.call-start = ((), (), s32[]{:S(2)}) async-start(), calls=%async_computation.4 | async-start | bytes 1179648 | tf_op jit(solution)/shard_map/reduce_scatter | solution.py:187
  (3 other events, 6.7 us)
Sparse Core Ops, SparseCore 0:
  112.3 54.1 all-reduce.1
  192.3 34.1 reduce-scatter.2
  229.4 32.6 reduce-scatter.4
